TPU v7x, 256 devices: a whole 4x4x8 slice. The times are simulated.
256 devices in a mesh: seq: 2 (over core), ctx: 64 (over x_lo, y, z), head: 2 (over x_hi).
Axes of the slice: x: 4 (x_hi: 2, x_lo: 2; x = x_hi * 2 + x_lo), y: 4, z: 8, core: 2. Of those that a mesh axis runs over, the one named last changes fastest.
Arguments:
- queries: bfloat16 [16384, 8, 128], P(('seq', 'ctx'), 'head'), parts along dimension 0, may hold values from -8 to 8
- key_rows: bfloat16 [16384, 128], P(('seq', 'ctx')), parts along dimension 0, may hold values from -8 to 8
- value_rows: bfloat16 [16384, 128], P(('seq', 'ctx')), parts along dimension 0, may hold values from -6 to 6
- out_grad: bfloat16 [16384, 8, 128], P(('seq', 'ctx'), 'head'), parts along dimension 0, may hold values from -6 to 6
- doc_lengths: int32 [16], P('seq'), parts along dimension 0, may hold values from 1 to 2048, 8192 in all
- balance: int32 [16384], P('seq'), parts along dimension 0, may hold values from 0 to 8191, as said below
Outputs:
- attended: bfloat16 [16384, 8, 128], P(('seq', 'ctx'), 'head'), parts along dimension 0
- query_grad: bfloat16 [16384, 8, 128], P(('seq', 'ctx'), 'head'), parts along dimension 0
- key_grad: bfloat16 [16384, 128], P(('seq', 'ctx')), parts along dimension 0
- value_grad: bfloat16 [16384, 128], P(('seq', 'ctx')), parts along dimension 0
There are 2 independent parts, one for each index of `seq`. A program takes and returns all parts, laid end to end along the dimension named above; each array names one. Nothing has to cross between parts.
Inputs may be any that keep to these rules, and one draw needn't show every extreme that they name: `doc_lengths`: the lengths sum to 8192 and the longest is exactly 2048. `balance`: A permutation of the positions that moves aligned runs of 64 positions whole and in order.
All inputs are finite; a program needn't handle non-finite values.
Results may differ from a plain program's by a relative error of at most 0.034.
Values may be sent and summed in bfloat16 or wider, within the bound.
A program may use at most 64 MiB of HBM per device.

v0:
```python
import math
import jax
import jax.numpy as jnp
from jax import lax
from jax.sharding import PartitionSpec as P

NEGATIVE = -1e30


def document_of(positions, doc_lengths):
    doc_ends = jnp.cumsum(doc_lengths)
    return jnp.sum((positions[:, None] >= doc_ends[None, :]).astype(jnp.int32), axis=1)


def body(queries, key_rows, value_rows, out_grad, doc_lengths, balance):
    tok_rows = queries.shape[0]
    heads_here = queries.shape[1]
    head_width = queries.shape[2]
    scaling = 1.0 / math.sqrt(head_width)
    seq_total = balance.shape[0]
    block_len = min(512, seq_total)
    block_count = seq_total // block_len
    docs_all = document_of(balance, doc_lengths)
    my_first = lax.axis_index("ctx") * tok_rows
    my_pos = lax.dynamic_slice_in_dim(balance, my_first, tok_rows)
    my_doc = lax.dynamic_slice_in_dim(docs_all, my_first, tok_rows)
    all_keys, all_values = (
        lax.all_gather(key_rows, "ctx", axis=0, tiled=True),
        lax.all_gather(value_rows, "ctx", axis=0, tiled=True),
    )

    def key_block(row_start):
        key_pos = lax.dynamic_slice_in_dim(balance, row_start, block_len)
        key_doc = lax.dynamic_slice_in_dim(docs_all, row_start, block_len)
        visible_pairs = (key_doc[None, :] == my_doc[:, None]) & (
            key_pos[None, :] <= my_pos[:, None]
        )
        key_blk = lax.dynamic_slice_in_dim(all_keys, row_start, block_len)
        value_blk = lax.dynamic_slice_in_dim(all_values, row_start, block_len)
        return (key_blk, value_blk, visible_pairs)

    def forward_step(step_index, state_now):
        key_blk, value_blk, visible_pairs = key_block(step_index * block_len)
        allowed = visible_pairs[:, None, :]
        running_max, weight_sum, weighted = state_now
        scores = (
            jnp.einsum("qhd,kd->qhk", queries, key_blk, preferred_element_type=jnp.float32)
            * scaling
        )
        scores = jnp.where(allowed, scores, NEGATIVE)
        new_max = jnp.maximum(running_max, jnp.max(scores, axis=2))
        raw_weights = jnp.where(allowed, jnp.exp(scores - new_max[:, :, None]), 0.0)
        factor = jnp.exp(running_max - new_max)
        weight_sum = weight_sum * factor + jnp.sum(raw_weights, axis=2)
        weighted = weighted * factor[:, :, None] + jnp.einsum(
            "qhk,kd->qhd",
            raw_weights.astype(jnp.bfloat16),
            value_blk,
            preferred_element_type=jnp.float32,
        )
        return (new_max, weight_sum, weighted)

    start_state = (
        jnp.full((tok_rows, heads_here), NEGATIVE, jnp.float32),
        jnp.zeros((tok_rows, heads_here), jnp.float32),
        jnp.zeros((tok_rows, heads_here, head_width), jnp.float32),
    )
    running_max, weight_sum, weighted = lax.fori_loop(0, block_count, forward_step, start_state)
    attended = (weighted / weight_sum[:, :, None]).astype(jnp.bfloat16)
    log_total = running_max + jnp.log(weight_sum)
    row_inner = jnp.sum(out_grad.astype(jnp.float32) * attended.astype(jnp.float32), axis=2)

    def backward_tile(query_part, grad_part, total_part, inner_part, key_blk, value_blk, allowed):
        scores = (
            jnp.einsum("qhd,kd->qhk", query_part, key_blk, preferred_element_type=jnp.float32)
            * scaling
        )
        weights = jnp.where(allowed, jnp.exp(scores - total_part[:, :, None]), 0.0)
        grad_weights = jnp.einsum(
            "qhd,kd->qhk", grad_part, value_blk, preferred_element_type=jnp.float32
        )
        grad_scores = (weights * (grad_weights - inner_part[:, :, None])).astype(jnp.bfloat16)
        return (weights.astype(jnp.bfloat16), grad_scores)

    def query_step(step_index, state_now):
        row_start = step_index * block_len
        key_blk, value_blk, visible_pairs = key_block(row_start)
        allowed = visible_pairs[:, None, :]
        grad_acc, key_terms = state_now
        weights_b, grad_scores = backward_tile(
            queries, out_grad, log_total, row_inner, key_blk, value_blk, allowed
        )
        grad_acc = grad_acc + jnp.einsum(
            "qhk,kd->qhd", grad_scores, key_blk, preferred_element_type=jnp.float32
        )
        key_part = (
            jnp.einsum("qhk,qhd->kd", grad_scores, queries, preferred_element_type=jnp.float32)
            * scaling
        )
        value_part = jnp.einsum(
            "qhk,qhd->kd", weights_b, out_grad, preferred_element_type=jnp.float32
        )
        key_terms = lax.dynamic_update_slice_in_dim(
            key_terms, jnp.concatenate([key_part, value_part], axis=1), row_start, 0
        )
        return (grad_acc, key_terms)

    grad_start = (
        jnp.zeros((tok_rows, heads_here, head_width), jnp.float32),
        jnp.zeros((seq_total, 2 * head_width), jnp.float32),
    )
    grad_acc, key_terms = lax.fori_loop(0, block_count, query_step, grad_start)
    query_grad = (grad_acc * scaling).astype(jnp.bfloat16)
    shared = lax.psum_scatter(key_terms, "ctx", scatter_dimension=0, tiled=True)
    combined = lax.psum(shared, "head")
    key_grad = combined[:, :head_width].astype(jnp.bfloat16)
    value_grad = combined[:, head_width:].astype(jnp.bfloat16)
    return (attended, query_grad, key_grad, value_grad)


def solution(mesh):
    return jax.shard_map(
        body,
        mesh=mesh,
        in_specs=(
            P(("seq", "ctx"), "head", None),
            P(("seq", "ctx"), None),
            P(("seq", "ctx"), None),
            P(("seq", "ctx"), "head", None),
            P("seq"),
            P("seq"),
        ),
        out_specs=(
            P(("seq", "ctx"), "head", None),
            P(("seq", "ctx"), "head", None),
            P(("seq", "ctx"), None),
            P(("seq", "ctx"), None),
        ),
        check_vma=False,
    )
```

profile of v0, /device:TPU:2, one launch (start us, length us, event | category | flops | bytes accessed | tf_op | source)
XLA Modules:
  0.0 1131.8 jit_solution(8781327198950465208)
XLA Ops:
  14.3 297.5 %all-gather.3.cloned.1.call-done = bf16[8192,128]{1,0:T(8,128)(2,1)} async-done(((bf16[128,128]{1,0:T(8,128)(2,1)}), bf16[8192,128]{1,0:T(8,128)(2,1)}) %all-gather.3.cloned.1.call-update) | async-done | bytes 2097168 | tf_op jit(solution)/shard_map/all_gather | solution.py:28
  311.8 299.0 %all-gather.5.cloned.1.call-done = bf16[8192,128]{1,0:T(8,128)(2,1)} async-done(((bf16[128,128]{1,0:T(8,128)(2,1)}), bf16[8192,128]{1,0:T(8,128)(2,1)}) %all-gather.5.cloned.1.call-update) | async-done | bytes 2097168 | tf_op jit(solution)/shard_map/all_gather | solution.py:29
  610.9 62.5 %while.34 = (s32[]{:T(128)}, f32[128,4]{0,1:T(4,128)S(1)}, f32[128,4]{0,1:T(4,128)S(1)}, f32[128,4,128]{2,0,1:T(8,128)S(1)}, s32[8192]{0:T(1024)S(1)}, /*index=5...) while((s32[]{:T(128)}, f32[128,4]{0,1:T(4,128)S(1)}, ...), condition=%wide.region_5.6_spmd.clone, body=%wide.region_2.5_spmd.clone.sunk | while | flops 136972800 | bytes 4371679 | solution.py:68
  613.4 1.3 convolution_add_fusion.4
  617.3 1.3 convolution_add_fusion.4
  621.2 1.3 convolution_add_fusion.4
  625.1 1.4 convolution_add_fusion.4
  629.0 1.3 convolution_add_fusion.4
  632.9 1.4 convolution_add_fusion.4
  636.8 1.3 convolution_add_fusion.4
  640.7 1.4 convolution_add_fusion.4
  644.6 1.3 convolution_add_fusion.4
  648.5 1.4 convolution_add_fusion.4
  652.4 1.3 convolution_add_fusion.4
  656.3 1.4 convolution_add_fusion.4
  660.2 1.3 convolution_add_fusion.4
  664.1 1.4 convolution_add_fusion.4
  668.0 1.3 convolution_add_fusion.4
  671.9 1.4 convolution_add_fusion.4
  674.4 3.8 broadcast_in_dim.114.clone
  678.2 104.2 %while.35 = (s32[]{:T(128)}, f32[128,4,128]{2,0,1:T(8,128)S(1)}, f32[8192,256]{1,0:T(8,128)}, s32[8192]{0:T(1024)S(1)}, s32[128]{0:T(128)S(1)}, /*index=5*/s32[8...) while((s32[]{:T(128)}, f32[128,4,128]{2,0,1:T(8,128)S(1)}, ...), condition=%wide.region_8.9_spmd.clone, body=%wide.region_7.8_spmd.clone.sunk | while | flops 337903616 | bytes 9979125 | solution.py:112
  679.3 1.2 fusion.81
  682.0 1.3 convolution_add_fusion.5
  688.5 1.3 convolution_add_fusion.5
  692.3 1.2 fusion.81
  695.0 1.3 convolution_add_fusion.5
  698.8 1.2 fusion.81
  701.6 1.3 convolution_add_fusion.5
  705.3 1.2 fusion.81
  708.1 1.3 convolution_add_fusion.5
  714.6 1.3 convolution_add_fusion.5
  718.3 1.2 fusion.81
  721.1 1.3 convolution_add_fusion.5
  727.6 1.3 convolution_add_fusion.5
  734.1 1.3 convolution_add_fusion.5
  737.9 1.2 fusion.81
  740.6 1.3 convolution_add_fusion.5
  744.4 1.2 fusion.81
  747.1 1.3 convolution_add_fusion.5
  753.7 1.3 convolution_add_fusion.5
  757.4 1.2 fusion.81
  760.2 1.3 convolution_add_fusion.5
  766.7 1.3 convolution_add_fusion.5
  773.2 1.3 convolution_add_fusion.5
  776.9 1.2 fusion.81
  779.7 1.3 convolution_add_fusion.5
  783.3 328.7 %reduce-scatter.2.cloned.1.call-done = f32[128,256]{1,0:T(8,128)} async-done(((f32[8192,256]{1,0:T(8,128)}), f32[128,256]{1,0:T(8,128)}) %reduce-scatter.2.cloned.1.call-update) | async-done | bytes 131088 | tf_op jit(solution)/shard_map/reduce_scatter | solution.py:114
  1112.0 12.7 %all-reduce.1 = bf16[128,256]{1,0:T(8,128)(2,1)S(1)} all-reduce(f32[128,256]{1,0:T(8,128)} %reduce-scatter.2.cloned.1.call-done), channel_id=1, replica_groups=mesh['seq'=2,'ctx'=64,'head'=2] {'head'}, use_global_device_ids=true, to_apply=%region_10.11 | all-reduce | flops 32768 | bytes 196608 | tf_op jit(solution)/shard_map/psum | solution.py:115
  (304 shorter events, 121.0 us)
Async XLA Ops:
  7.2 304.7 %all-gather.3.cloned.1.call-start = ((), (), s32[]{:S(2)}) async-start(), calls=%async_computation.1 | async-start | bytes 2129920 | tf_op jit(solution)/shard_map/all_gather | solution.py:28
  7.9 603.0 %all-gather.5.cloned.1.call-start = ((), (), s32[]{:S(2)}) async-start(), calls=%async_computation.2 | async-start | bytes 2129920 | tf_op jit(solution)/shard_map/all_gather | solution.py:29
  8.6 1103.4 %reduce-scatter.2.cloned.1.call-start = ((), (), s32[]{:S(2)}) async-start(), calls=%async_computation.3 | async-start | bytes 8519680 | tf_op jit(solution)/shard_map/reduce_scatter | solution.py:114
  610.9 62.6 %copy-start = (bf16[128,4,128]{2,1,0:T(4,128)(2,1)S(1)}, bf16[128,4,128]{2,1,0:T(4,128)(2,1)}, u32[]{:S(2)}) copy-start(bf16[128,4,128]{2,1,0:T(4,128)(2,1)} %param.13) | copy-start | bytes 393220
Sparse Core Ops, SparseCore 0:
  9.8 301.9 all-gather.2
  313.6 297.2 all-gather.4
  782.6 329.3 reduce-scatter.1
where the time goes:
time: 1130 us
  waiting for transfers between devices  927 us (82%)
  matrix products  110 us (10%)
  local copies, waits for them, and re-layouts  51.9 us (5%)
  other arithmetic  14.3 us (1%)
  between operations  13.8 us (1%)
  blocking collectives  12.7 us (1%)
    reduce_scatter x1, waiting for transfers between devices, body(): shared = lax.psum_scatter(key_terms, 'ctx', scatter_dimension=0, tiled=True)  329 us
    all_gather x1, waiting for transfers between devices, body(): lax.all_gather(value_rows, 'ctx', axis=0, tiled=True)  299 us
    all_gather x1, waiting for transfers between devices, body(): lax.all_gather(key_rows, 'ctx', axis=0, tiled=True)  297 us
    dynamic_slice x32, local copies, waits for them, and re-layouts, key_block(): key_pos = lax.dynamic_slice_in_dim(balance, row_start, block_len)  24.4 us
  transfers between devices with their start and end apart: 3, of which 3 were waited for; matrix products, arithmetic and copies ran while one was open for 1% of the time, Pallas kernels for 0%

commit v1 on v0

--- a/solution.py
+++ b/solution.py
@@ -26,7 +26,9 @@
     my_doc = lax.dynamic_slice_in_dim(docs_all, my_first, tok_rows)
     all_keys, all_values = (
         lax.all_gather(key_rows, "ctx", axis=0, tiled=True),
-        lax.all_gather(value_rows, "ctx", axis=0, tiled=True),
+        jnp.concatenate(
+            lax.all_to_all(jnp.stack([value_rows] * lax.axis_size("ctx")), "ctx", 0, 0), axis=0
+        ),
     )
 
     def key_block(row_start):

time: 1130 us -> 850 us (0.75)
  waiting for transfers between devices: 927 us -> 617 us
  local copies, waits for them, and re-layouts: 51.9 us -> 75 us
  starting transfers between devices: 0.11 us -> 13.4 us
  matrix products: 110 us -> 97 us
    all_gather x1 -> x0, waiting for transfers between devices: 299 us -> none  [body(): lax.all_gather(value_rows, 'ctx', axis=0, tiled=True)]
    dynamic_slice x32, local copies, waits for them, and re-layouts: 2.37 us -> 24.3 us  [key_block(): key_doc = lax.dynamic_slice_in_dim(docs_all, row_start, block_len)]
    dot_general x16, matrix products: 19.1 us -> 4.52 us  [backward_tile(): jnp.einsum('qhd,kd->qhk', grad_part, value_blk, preferred_element_type=jn...]
    dot_general x16, matrix products: 21.6 us -> 7.14 us  [forward_step(): jnp.einsum('qhk,kd->qhd', raw_weights.astype(jnp.bfloat16), value_blk, pr...]
    dot_general x16, matrix products: 4.93 us -> 19.4 us  [query_step(): jnp.einsum('qhk,qhd->kd', grad_scores, queries, preferred_element_type=jn...]
    all_to_all x0 -> x1, starting transfers between devices: none -> 13.3 us  [body(): lax.all_to_all(jnp.stack([value_rows] * lax.axis_size('ctx')), 'ctx', 0, 0)]
  transfers between devices with their start and end apart: 3 -> 3, of which waited for: 3 -> 2; matrix products, arithmetic and copies ran while one was open for 1% -> 1% of each run, Pallas kernels for 0% -> 0%
where the time goes in v1:
time: 850 us; the launch traced here: 846 us
  waiting for transfers between devices  617 us (73%)
  matrix products  97 us (11%)
  local copies, waits for them, and re-layouts  75 us (9%)
  other arithmetic  14.3 us (2%)
  between operations  14.1 us (2%)
  blocking collectives  13.8 us (2%)
  starting transfers between devices  13.4 us (2%)
    reduce_scatter x1, waiting for transfers between devices, body(): shared = lax.psum_scatter(key_terms, 'ctx', scatter_dimension=0, tiled=True)  328 us
    all_gather x1, waiting for transfers between devices, body(): lax.all_gather(key_rows, 'ctx', axis=0, tiled=True)  288 us
    dynamic_slice x32, local copies, waits for them, and re-layouts, key_block(): key_pos = lax.dynamic_slice_in_dim(balance, row_start, block_len)  24.4 us
    dynamic_slice x32, local copies, waits for them, and re-layouts, key_block(): key_doc = lax.dynamic_slice_in_dim(docs_all, row_start, block_len)  24.3 us
    dot_general x16, matrix products, backward_tile(): jnp.einsum('qhd,kd->qhk', query_part, key_blk, preferred_element_type=jnp...  21 us
    dot_general x16, matrix products, query_step(): jnp.einsum('qhk,kd->qhd', grad_scores, key_blk, preferred_element_type=jn...  20.5 us
    dot_general x16, matrix products, forward_step(): jnp.einsum('qhd,kd->qhk', queries, key_blk, preferred_element_type=jnp.fl...  19.6 us
    dot_general x16, matrix products, query_step(): jnp.einsum('qhk,qhd->kd', grad_scores, queries, preferred_element_type=jn...  19.4 us
  transfers between devices with their start and end apart: 3, of which 2 were waited for; matrix products, arithmetic and copies ran while one was open for 1% of the time, Pallas kernels for 0%

profile of v1, /device:TPU:2, one launch (start us, length us, event | category | flops | bytes accessed | tf_op | source)
XLA Modules:
  0.0 846.3 jit_solution(11324856530323034440)
XLA Ops:
  7.9 2.6 stack.2
  10.5 13.3 %all-to-all-start = ((bf16[64,128,128]{2,1,0:T(8,128)(2,1)}), bf16[64,128,128]{2,1,0:T(8,128)(2,1)S(1)}, u32[]{:S(2)}, u32[]{:S(2)}) async-start(bf16[64,128,128]{2,1,0:T(8,128)(2,1)} %stack.2), calls=%async_computation | async-start | bytes 4194304 | tf_op jit(solution)/shard_map/all_to_all | solution.py:30
  25.7 1.5 convert_reduce_fusion
  28.1 288.3 %all-gather.2.cloned.1.call-done = bf16[8192,128]{1,0:T(8,128)(2,1)} async-done(((bf16[128,128]{1,0:T(8,128)(2,1)}), bf16[8192,128]{1,0:T(8,128)(2,1)}) %all-gather.2.cloned.1.call-update) | async-done | bytes 2097168 | tf_op jit(solution)/shard_map/all_gather | solution.py:28
  316.4 59.0 %while.34 = (s32[]{:T(128)}, f32[128,4]{0,1:T(4,128)S(1)}, f32[128,4]{0,1:T(4,128)S(1)}, f32[128,4,128]{2,0,1:T(8,128)S(1)}, s32[8192]{0:T(1024)}, /*index=5*/s3...) while((s32[]{:T(128)}, f32[128,4]{0,1:T(4,128)S(1)}, ...), condition=%wide.region_5.6_spmd.clone, body=%wide.region_2.5_spmd.clone.sunk | while | flops 136972800 | bytes 4371679 | solution.py:70
  321.8 1.2 fusion.68
  325.5 1.2 fusion.68
  329.2 1.2 fusion.68
  332.9 1.2 fusion.68
  336.6 1.2 fusion.68
  340.3 1.2 fusion.68
  344.0 1.2 fusion.68
  376.5 3.8 broadcast_in_dim.114.clone
  380.3 116.0 %while.35 = (s32[]{:T(128)}, f32[128,4,128]{2,0,1:T(8,128)S(1)}, f32[8192,256]{1,0:T(8,128)}, s32[8192]{0:T(1024)}, s32[128]{0:T(128)S(1)}, /*index=5*/s32[8192]...) while((s32[]{:T(128)}, f32[128,4,128]{2,0,1:T(8,128)S(1)}, ...), condition=%wide.region_8.9_spmd.clone, body=%wide.region_7.8_spmd.clone.sunk | while | flops 337903616 | bytes 9979125 | solution.py:114
  382.0 1.3 fusion.81
  384.0 1.3 convolution_add_fusion.5
  389.3 1.3 fusion.81
  391.2 1.3 convolution_add_fusion.5
  396.5 1.3 fusion.81
  398.5 1.3 convolution_add_fusion.5
  403.8 1.3 fusion.81
  405.7 1.3 convolution_add_fusion.5
  411.1 1.3 fusion.81
  413.0 1.3 convolution_add_fusion.5
  418.3 1.3 fusion.81
  420.2 1.3 convolution_add_fusion.5
  425.6 1.3 fusion.81
  427.5 1.3 convolution_add_fusion.5
  432.8 1.3 fusion.81
  434.7 1.3 convolution_add_fusion.5
  440.1 1.3 fusion.81
  442.0 1.3 convolution_add_fusion.5
  447.3 1.3 fusion.81
  449.2 1.3 convolution_add_fusion.5
  454.6 1.3 fusion.81
  456.5 1.3 convolution_add_fusion.5
  461.8 1.3 fusion.81
  463.7 1.3 convolution_add_fusion.5
  469.1 1.3 fusion.81
  471.0 1.3 convolution_add_fusion.5
  476.3 1.3 fusion.81
  478.2 1.3 convolution_add_fusion.5
  483.6 1.3 fusion.81
  485.5 1.3 convolution_add_fusion.5
  490.8 1.3 fusion.81
  492.7 1.3 convolution_add_fusion.5
  497.2 327.7 %reduce-scatter.2.cloned.1.call-done = f32[128,256]{1,0:T(8,128)} async-done(((f32[8192,256]{1,0:T(8,128)}), f32[128,256]{1,0:T(8,128)}) %reduce-scatter.2.cloned.1.call-update) | async-done | bytes 131088 | tf_op jit(solution)/shard_map/reduce_scatter | solution.py:116
  824.9 13.8 %all-reduce.1 = bf16[128,256]{1,0:T(8,128)(2,1)S(1)} all-reduce(f32[128,256]{1,0:T(8,128)} %reduce-scatter.2.cloned.1.call-done), channel_id=1, replica_groups=mesh['seq'=2,'ctx'=64,'head'=2] {'head'}, use_global_device_ids=true, to_apply=%region_10.11 | all-reduce | flops 32768 | bytes 196608 | tf_op jit(solution)/shard_map/psum | solution.py:117
  (308 shorter events, 129.0 us)
Async XLA Ops:
  7.2 309.3 %all-gather.2.cloned.1.call-start = ((), (), s32[]{:S(2)}) async-start(), calls=%async_computation.2 | async-start | bytes 2129920 | tf_op jit(solution)/shard_map/all_gather | solution.py:28
  10.5 13.4 %copy-start.1 = (bf16[128,4,128]{2,1,0:T(4,128)(2,1)S(1)}, bf16[128,4,128]{2,1,0:T(4,128)(2,1)}, u32[]{:S(2)}) copy-start(bf16[128,4,128]{2,1,0:T(4,128)(2,1)} %param.10) | copy-start | bytes 393220
  10.5 14.3 %copy-start.2 = (s32[8]{0:T(128)S(1)}, s32[8]{0:T(128)}, u32[]{:S(2)}) copy-start(s32[8]{0:T(128)} %param.14) | copy-start | bytes 100
  10.5 17.5 %copy-start = (bf16[128,4,128]{2,1,0:T(4,128)(2,1)S(1)}, bf16[128,4,128]{2,1,0:T(4,128)(2,1)}, u32[]{:S(2)}) copy-start(bf16[128,4,128]{2,1,0:T(4,128)(2,1)} %param.13) | copy-start | bytes 393220
  10.5 305.9 %all-to-all-start = ((bf16[64,128,128]{2,1,0:T(8,128)(2,1)}), bf16[64,128,128]{2,1,0:T(8,128)(2,1)S(1)}, u32[]{:S(2)}, u32[]{:S(2)}) async-start(bf16[64,128,128]{2,1,0:T(8,128)(2,1)} %stack.2), calls=%async_computation | async-start | bytes 4194304 | tf_op jit(solution)/shard_map/all_to_all | solution.py:30
  23.9 801.1 %reduce-scatter.2.cloned.1.call-start = ((), (), s32[]{:S(2)}) async-start(), calls=%async_computation.3 | async-start | bytes 8519680 | tf_op jit(solution)/shard_map/reduce_scatter | solution.py:116
Sparse Core Ops, SparseCore 0:
  9.8 306.5 all-gather.1
  496.5 328.4 reduce-scatter.1
